TPU v7x, 128 devices: a whole 4x4x4 slice. The times are simulated.
128 devices in a mesh: dp: 32 (over x, z, core), rep: 4 (over y).
Axes of the slice: x: 4, y: 4, z: 4, core: 2. Of those that a mesh axis runs over, the one named last changes fastest.
Arguments:
- cross_in: bfloat16 [65536, 3456], P(('dp', 'rep')), may hold values from -24 to 24
- cotangent: bfloat16 [65536, 3456], P(('dp', 'rep')), may hold values from -24 to 24
- weight_down: bfloat16 [3456, 512], replicated, may hold values from -0.109375 to 0.109375
- weight_up: bfloat16 [512, 3456], replicated, may hold values from -0.25 to 0.25
- cross_bias: float32 [3456], replicated, may hold values from -3 to 3
- row_place: int32 [65536, 26], P(('dp', 'rep')), may hold values from 0 to 66559, as said below
- frequent_table: float32 [1024, 128], replicated, may hold values from -0.6 to 0.6
- frequent_accum: float32 [1024], replicated, may hold values from 416 to 106496
- shard_table: float32 [65536, 128], P('dp'), may hold values from -0.6 to 0.6
- shard_accum: float32 [65536], P('dp'), may hold values from 0.01 to 1
Outputs:
- new_frequent: float32 [1024, 128], replicated
- new_frequent_accum: float32 [1024], replicated
- new_shard: float32 [65536, 128], P('dp')
- new_shard_accum: float32 [65536], P('dp')
- grad_up: float32 [512, 3456], P(('dp', 'rep'))
- grad_down: float32 [3456, 512], P(('dp', 'rep'))
- grad_bias: float32 [3456], P(('dp', 'rep'))
Inputs may be any that keep to these rules, and one draw needn't show every extreme that they name: `row_place`: within the rows of one device (aligned blocks of 512 samples), at most 208 entries name rows of any one owner, and in every block some owner is named by exactly 208 entries; every owner is named at least once in every block.
All inputs are finite; a program needn't handle non-finite values.
Results may differ from a plain program's by a relative error of at most 0.0013.
The roundings to bfloat16 on the way count: a program that leaves them out, or rounds other values in their place, can miss the bound.
Values sent between devices are 32-bit elements; how exact they have to be, the bound alone decides.
A program may use at most 192 MiB of HBM per device.

v0:
```python
import jax
import jax.numpy as jnp
from jax import lax
from jax.sharding import PartitionSpec as P

learn_rate = 0.05
eps_ada = 1e-08


def row_adagrad(table, accum, grad):
    accum_new = accum + jnp.mean(grad * grad, axis=1)
    return (table - learn_rate * grad / (jnp.sqrt(accum_new)[:, None] + eps_ada), accum_new)


def body(
    cross_in,
    cotangent,
    weight_down,
    weight_up,
    cross_bias,
    row_place,
    frequent_table,
    frequent_accum,
    shard_table,
    shard_accum,
):
    emb_width = frequent_table.shape[1]
    num_tables = row_place.shape[1]
    local_rows = cross_in.shape[0]
    f_count = frequent_table.shape[0]
    owned_rows = shard_table.shape[0]
    hidden = jnp.dot(cross_in, weight_down, preferred_element_type=jnp.float32).astype(jnp.bfloat16)
    scaled = jnp.dot(hidden, weight_up, preferred_element_type=jnp.float32) + cross_bias
    cot_wide = cotangent.astype(jnp.float32)
    inner = cot_wide * cross_in.astype(jnp.float32)
    inner_half = inner.astype(jnp.bfloat16)
    back_low = lax.dot_general(
        inner_half, weight_up, (((1,), (1,)), ((), ())), preferred_element_type=jnp.float32
    ).astype(jnp.bfloat16)
    back_in = cot_wide * (scaled + 1.0) + lax.dot_general(
        back_low, weight_down, (((1,), (1,)), ((), ())), preferred_element_type=jnp.float32
    )
    local_up = lax.dot_general(
        hidden, inner_half, (((0,), (0,)), ((), ())), preferred_element_type=jnp.float32
    )
    local_down = lax.dot_general(
        cross_in, back_low, (((0,), (0,)), ((), ())), preferred_element_type=jnp.float32
    )
    local_bias = jnp.sum(inner, axis=0)
    grad_up, grad_down, grad_bias = (
        lax.psum_scatter(local_up, ("dp", "rep"), scatter_dimension=0, tiled=True),
        lax.psum_scatter(local_down, ("dp", "rep"), scatter_dimension=0, tiled=True),
        lax.psum_scatter(local_bias, ("dp", "rep"), scatter_dimension=0, tiled=True),
    )
    values = back_in[:, emb_width:].reshape(local_rows * num_tables, emb_width)
    places = row_place.reshape(-1)
    is_frequent = places < f_count
    freq_grad = jax.ops.segment_sum(values, jnp.where(is_frequent, places, f_count), f_count + 1)[
        :f_count
    ]
    shards = lax.axis_size("dp")
    capacity = local_rows * num_tables // (2 * shards)
    owners = jnp.where(is_frequent, shards, (places - f_count) // owned_rows)
    owner_row = jnp.where(is_frequent, 0, (places - f_count) % owned_rows)
    sorted_order = jnp.argsort(owners, stable=True)
    sorted_owner = owners[sorted_order]
    counts = jnp.sum((owners[:, None] == jnp.arange(shards + 1)[None, :]).astype(jnp.int32), axis=0)
    starts = jnp.cumsum(counts) - counts
    slot_pos = jnp.arange(owners.shape[0]) - starts[sorted_owner]
    target = jnp.where(sorted_owner < shards, sorted_owner * capacity + slot_pos, shards * capacity)
    bucket = (
        jnp.zeros((shards * capacity + 1, emb_width), jnp.float32)
        .at[target]
        .set(values[sorted_order])
    )
    bucket = bucket[: shards * capacity].reshape(shards, capacity, emb_width)
    bucket_rows = (
        jnp.zeros((shards * capacity + 1,), jnp.int32).at[target].set(owner_row[sorted_order])
    )
    bucket_rows = bucket_rows[: shards * capacity].reshape(shards, capacity)
    arrived, arrived_rows = (
        lax.all_to_all(bucket, "dp", split_axis=0, concat_axis=0, tiled=True),
        lax.all_to_all(bucket_rows, "dp", split_axis=0, concat_axis=0, tiled=True),
    )
    shard_grad = jax.ops.segment_sum(
        arrived.reshape(-1, emb_width), arrived_rows.reshape(-1), owned_rows
    )
    shard_grad = lax.psum(shard_grad, "rep")
    new_shard, new_shard_accum = row_adagrad(shard_table, shard_accum, shard_grad)
    freq_total = lax.psum(freq_grad, ("dp", "rep"))
    new_frequent, new_frequent_accum = row_adagrad(frequent_table, frequent_accum, freq_total)
    return (
        new_frequent,
        new_frequent_accum,
        new_shard,
        new_shard_accum,
        grad_up,
        grad_down,
        grad_bias,
    )


def solution(mesh):
    in_specs = (
        P(("dp", "rep"), None),
        P(("dp", "rep"), None),
        P(),
        P(),
        P(),
        P(("dp", "rep"), None),
        P(),
        P(),
        P("dp", None),
        P("dp"),
    )
    out_specs = (
        P(),
        P(),
        P("dp", None),
        P("dp"),
        P(("dp", "rep"), None),
        P(("dp", "rep"), None),
        P(("dp", "rep")),
    )
    return jax.shard_map(body, mesh=mesh, in_specs=in_specs, out_specs=out_specs, check_vma=False)
```

profile of v0, /device:TPU:1, one launch (start us, length us, event | category | flops | bytes accessed | tf_op | source)
XLA Modules:
  0.0 876.3 jit_solution(13880018079292635862)
XLA Ops:
  22.4 9.1 %sort.17 = (s32[13312]{0:T(1024)}, s32[13312]{0:T(1024)}) sort(s32[13312]{0:T(1024)} %copy-done.2, s32[13312]{0:T(1024)} %iota.12), dimensions={0}, to_apply=%region_3.0 | sort | flops 186368 | bytes 212992 | tf_op jit(solution)/shard_map/jit(argsort)/sort | solution.py:65
  32.9 121.2 %gather_fusion = s32[13312]{0:T(1024)} fusion(s32[13312]{0:T(1024)} %copy-done.2, s32[13312]{0:T(1024)} %fusion.19), kind=kCustom, calls=%fused_computation | custom fusion | bytes 159744 | tf_op jit(solution)/shard_map/gather | solution.py:66
  154.1 5.3 compare_select_fusion.3
  159.4 4.2 compare_reduce_fusion.25
  163.7 16.6 %select_select_fusion = s32[13312]{0:T(1024)S(1)} fusion(pred[13312]{0:T(1024)(128)(4,1)S(1)} %get-tuple-element.62, pred[13312]{0:T(1024)(128)(4,1)S(1)} %get-tuple-element.61, pred[13312]{0:T(1024)(128)(4,1)S(1)} %get-tuple-element.60, pred[13312]{0:T(1024)(128)(4,1)S(1)} %get-tuple-element.59, pred[13312]{0:T(1024)(128)(4,1)S(1)} %get-tuple-element.58, ...), kind=kLoop, calls=%fused_computation.77 | loop fusion | flops 346112 | bytes 452712 | tf_op jit(solution)/shard_map/gather | solution.py:69
  181.8 120.7 %gather_fusion.1 = s32[13312]{0:T(1024)} fusion(s32[13312]{0:T(1024)} %get-tuple-element.72, s32[13312]{0:T(1024)} %fusion.19), kind=kCustom, calls=%fused_computation.1 | custom fusion | bytes 159744 | tf_op jit(solution)/shard_map/gather | solution.py:78
  302.6 49.8 %scatter_custom_fusion.1 = s32[6657]{0:T(1024)} fusion(s32[13312]{0:T(1024)} %bitcast.62, s32[13312]{0:T(1024)} %gather_fusion.1, s32[]{:T(128)} %constant.29.clone.1), kind=kCustom, calls=%fused_computation.83 | custom fusion | bytes 27140 | tf_op jit(solution)/shard_map/scatter | solution.py:78
  353.9 9.8 %all-to-all-start = ((s32[32,1,208]{2,1,0:T(1,128)}), s32[32,1,208]{2,1,0:T(1,128)}, u32[]{:S(2)}, u32[]{:S(2)}) async-start(s32[32,1,208]{2,1,0:T(1,128)} %all_to_all.9), calls=%async_computation | async-start | bytes 65536 | tf_op jit(solution)/shard_map/all_to_all | solution.py:83
  363.7 2.6 convert_element_type.18
  369.9 2.1 fusion.10
  374.3 2.1 fusion.27
  376.4 3.3 slice_add_fusion
  379.7 7.8 reshape.231
  387.5 108.6 %scatter_custom_fusion.2 = f32[6657,128]{1,0:T(8,128)S(1)} fusion(s32[13312]{0:T(1024)} %bitcast.63, f32[13312,128]{1,0:T(8,128)} %reshape.231, s32[13312]{0:T(1024)} %fusion.19, f32[]{:T(128)} %constant.21.clone.1), kind=kCustom, calls=%fused_computation.12 | custom fusion | bytes 3408896 | tf_op jit(solution)/shard_map/scatter | solution.py:74
  498.2 7.8 all-to-all-start.1
  511.1 72.4 %scatter_custom_fusion = f32[1025,128]{1,0:T(8,128)} fusion(s32[13312]{0:T(1024)} %bitcast.64, f32[13312,128]{1,0:T(8,128)} %reshape.231, f32[]{:T(128)} %constant.21.clone.1), kind=kCustom, calls=%fused_computation.33 | custom fusion | flops 1703936 | bytes 525312 | tf_op jit(solution)/shard_map/scatter-add | solution.py:58
  588.2 41.0 %scatter_custom_fusion.3 = f32[2048,128]{1,0:T(8,128)} fusion(s32[6656]{0:T(1024)} %reshape.253, f32[6656,128]{1,0:T(8,128)} %bitcast.40, f32[]{:T(128)} %constant.21.clone.1), kind=kCustom, calls=%fused_computation.26 | custom fusion | flops 851968 | bytes 1049088 | tf_op jit(solution)/shard_map/scatter-add | solution.py:85
  629.4 6.2 convolution_bitcast_fusion
  635.6 5.1 fusion.6
  640.7 4.2 fusion.3
  644.8 67.5 %all-reduce.2 = f32[3456]{0:T(1024)} all-reduce(f32[3456]{0:T(1024)S(1)} %fusion.3), channel_id=4, replica_groups=mesh['dp'=32,'rep'=4] {'dp','rep'}, use_global_device_ids=true, to_apply=%region_14.15.clone | all-reduce | flops 3456 | bytes 27648
  716.5 3.0 divide_subtract_fusion
  719.4 140.0 %all-reduce.9.cloned.1.call-done = (f32[1024,128]{1,0:T(8,128)}, f32[512,3456]{1,0:T(8,128)}, f32[3456,512]{0,1:T(8,128)}) async-done(((f32[1024,128]{1,0:T(8,128)}, f32[512,3456]{1,0:T(8,128)}, f32[3456,512]{0,1:T(8,128)}), (f32[1024,128]{1,0:T(8,128)}, f32[512,3456]{1,0:T(8,128)}, f32[3456,512]{0,1:T(8,128)})) %all-reduce.9.cloned.1.call-update) | async-done | bytes 14680080 | tf_op jit(solution)/shard_map/psum | solution.py:90
  865.5 2.2 divide_subtract_fusion.1
  (69 shorter events, 49.2 us)
Async XLA Ops:
  7.2 362.8 %copy-start = (bf16[512,3456]{1,0:T(8,128)(2,1)S(1)}, bf16[512,3456]{1,0:T(8,128)(2,1)}, u32[]{:S(2)}) copy-start(bf16[512,3456]{1,0:T(8,128)(2,1)} %param.13) | copy-start | bytes 10616836
  16.4 0.6 copy-start.2
  353.9 144.3 %all-to-all-start = ((s32[32,1,208]{2,1,0:T(1,128)}), s32[32,1,208]{2,1,0:T(1,128)}, u32[]{:S(2)}, u32[]{:S(2)}) async-start(s32[32,1,208]{2,1,0:T(1,128)} %all_to_all.9), calls=%async_computation | async-start | bytes 65536 | tf_op jit(solution)/shard_map/all_to_all | solution.py:83
  363.7 3.1 copy-start.3
  363.7 4.1 copy-start.7
  367.9 2.1 copy-start.5
  369.9 2.1 copy-start.9
  372.1 4.3 copy-start.11
  372.1 2.2 copy-start.8
  374.3 2.1 copy-start.12
  498.2 131.1 %copy-start.4 = (bf16[512,3456]{1,0:T(8,128)(2,1)S(1)}, bf16[512,3456]{1,0:T(8,128)(2,1)}, u32[]{:S(2)}) copy-start(bf16[512,3456]{1,0:T(8,128)(2,1)} %param.10) | copy-start | bytes 10616836
  498.2 90.0 %all-to-all-start.1 = ((f32[32,208,128]{2,1,0:T(8,128)}), f32[32,208,128]{2,1,0:T(8,128)}, u32[]{:S(2)}, u32[]{:S(2)}) async-start(f32[32,208,128]{2,1,0:T(8,128)} %bitcast.56), calls=%async_computation.1 | async-start | bytes 6815744 | tf_op jit(solution)/shard_map/all_to_all | solution.py:82
  506.1 207.5 %all-reduce.7.cloned.1.call-start = ((), (), s32[]{:S(2)}) async-start(), calls=%async_computation.2 | async-start | bytes 2097152 | tf_op jit(solution)/shard_map/psum | solution.py:88
  629.3 230.1 %all-reduce.9.cloned.1.call-start = ((), (), s32[]{:S(2)}) async-start(), calls=%async_computation.3 | async-start | bytes 29360128 | tf_op jit(solution)/shard_map/psum | solution.py:90
  629.3 6.2 copy-start.6
  629.4 6.2 copy-start.10
  640.7 228.6 %copy-start.1 = (bf16[512,3456]{1,0:T(8,128)(2,1)S(1)}, bf16[512,3456]{1,0:T(8,128)(2,1)}, u32[]{:S(2)}) copy-start(bf16[512,3456]{1,0:T(8,128)(2,1)} %param.13) | copy-start | bytes 10616836
Sparse Core Ops, SparseCore 0:
  629.4 46.4 all-reduce.6
  683.0 176.4 all-reduce.8
where the time goes:
time: 884 us; the launch traced here: 876 us
  local copies, waits for them, and re-layouts  435 us (49%)
  other arithmetic  182 us (21%)
  waiting for transfers between devices  140 us (16%)
  blocking collectives  67.5 us (8%)
  matrix products  19.6 us (2%)
  starting transfers between devices  17.8 us (2%)
  between operations  14.5 us (2%)
    psum x1, waiting for transfers between devices, body(): freq_total = lax.psum(freq_grad, ('dp', 'rep'))  140 us
    gather x1, local copies, waits for them, and re-layouts, body(): sorted_owner = owners[sorted_order]  121 us
    gather x1, local copies, waits for them, and re-layouts, body(): owner_row[sorted_order]  121 us
    scatter x1, local copies, waits for them, and re-layouts, body(): bucket = jnp.zeros((shards * capacity + 1, emb_width), jnp.float32).at[ta...  109 us
    scatter-add x1, other arithmetic, body(): jax.ops.segment_sum(values, jnp.where(is_frequent, places, f_count), f_co...  72.4 us
    unnamed x1, blocking collectives  67.5 us
    scatter x1, local copies, waits for them, and re-layouts, body(): jnp.zeros((shards * capacity + 1,), jnp.int32).at[target]  49.8 us
    scatter-add x1, other arithmetic, body(): jax.ops.segment_sum(arrived.reshape(-1, emb_width), arrived_rows.reshape(...  41 us
  transfers between devices with their start and end apart: 4, of which 1 were waited for; matrix products, arithmetic and copies ran while one was open for 27% of the time, Pallas kernels for 0%

commit v1 on v0

--- a/solution.py
+++ b/solution.py
@@ -87,7 +87,7 @@
     )
     shard_grad = lax.psum(shard_grad, "rep")
     new_shard, new_shard_accum = row_adagrad(shard_table, shard_accum, shard_grad)
-    freq_total = lax.psum(freq_grad, ("dp", "rep"))
+    freq_total = lax.psum(lax.psum(freq_grad, "dp"), "rep")
     new_frequent, new_frequent_accum = row_adagrad(frequent_table, frequent_accum, freq_total)
     return (
         new_frequent,

time: 884 us -> 943 us (1.067)
  waiting for transfers between devices: 140 us -> 199 us
    unnamed x2 -> x4, waiting for transfers between devices: 0.03 us -> 138 us
    psum x2, waiting for transfers between devices: 140 us -> 61 us  [body(): freq_total = lax.psum(lax.psum(freq_grad, 'dp'), 'rep')]
  transfers between devices with their start and end apart: 4 -> 5, of which waited for: 1 -> 2; matrix products, arithmetic and copies ran while one was open for 27% -> 30% of each run, Pallas kernels for 0% -> 0%
where the time goes in v1:
time: 943 us; the launch traced here: 934 us
  local copies, waits for them, and re-layouts  435 us (46%)
  waiting for transfers between devices  199 us (21%)
  other arithmetic  182 us (19%)
  blocking collectives  66.6 us (7%)
  matrix products  19.6 us (2%)
  starting transfers between devices  17.8 us (2%)
  between operations  14.2 us (2%)
    unnamed x4, waiting for transfers between devices  138 us
    gather x1, local copies, waits for them, and re-layouts, body(): sorted_owner = owners[sorted_order]  121 us
    gather x1, local copies, waits for them, and re-layouts, body(): owner_row[sorted_order]  121 us
    scatter x1, local copies, waits for them, and re-layouts, body(): bucket = jnp.zeros((shards * capacity + 1, emb_width), jnp.float32).at[ta...  109 us
    scatter-add x1, other arithmetic, body(): jax.ops.segment_sum(values, jnp.where(is_frequent, places, f_count), f_co...  72.4 us
    unnamed x1, blocking collectives  66.6 us
    psum x2, waiting for transfers between devices, body(): freq_total = lax.psum(lax.psum(freq_grad, 'dp'), 'rep')  61 us
    scatter x1, local copies, waits for them, and re-layouts, body(): jnp.zeros((shards * capacity + 1,), jnp.int32).at[target]  49.8 us
  transfers between devices with their start and end apart: 5, of which 2 were waited for; matrix products, arithmetic and copies ran while one was open for 30% of the time, Pallas kernels for 0%

profile of v1, /device:TPU:1, one launch (start us, length us, event | category | flops | bytes accessed | tf_op | source)
XLA Modules:
  0.0 934.4 jit_solution(16993837803218732902)
XLA Ops:
  22.4 9.1 sort.17
  32.9 121.2 %gather_fusion = s32[13312]{0:T(1024)} fusion(s32[13312]{0:T(1024)} %copy-done.2, s32[13312]{0:T(1024)} %fusion.19), kind=kCustom, calls=%fused_computation | custom fusion | bytes 159744 | tf_op jit(solution)/shard_map/gather | solution.py:66
  154.1 5.3 compare_select_fusion.3
  159.4 4.2 compare_reduce_fusion.25
  163.7 16.6 %select_select_fusion = s32[13312]{0:T(1024)S(1)} fusion(pred[13312]{0:T(1024)(128)(4,1)S(1)} %get-tuple-element.62, pred[13312]{0:T(1024)(128)(4,1)S(1)} %get-tuple-element.61, pred[13312]{0:T(1024)(128)(4,1)S(1)} %get-tuple-element.60, pred[13312]{0:T(1024)(128)(4,1)S(1)} %get-tuple-element.59, pred[13312]{0:T(1024)(128)(4,1)S(1)} %get-tuple-element.58, ...), kind=kLoop, calls=%fused_computation.77 | loop fusion | flops 346112 | bytes 452712 | tf_op jit(solution)/shard_map/gather | solution.py:69
  181.8 120.7 %gather_fusion.1 = s32[13312]{0:T(1024)} fusion(s32[13312]{0:T(1024)} %get-tuple-element.73, s32[13312]{0:T(1024)} %fusion.19), kind=kCustom, calls=%fused_computation.1 | custom fusion | bytes 159744 | tf_op jit(solution)/shard_map/gather | solution.py:78
  302.6 49.8 %scatter_custom_fusion.1 = s32[6657]{0:T(1024)} fusion(s32[13312]{0:T(1024)} %bitcast.62, s32[13312]{0:T(1024)} %gather_fusion.1, s32[]{:T(128)} %constant.29.clone.1), kind=kCustom, calls=%fused_computation.83 | custom fusion | bytes 27140 | tf_op jit(solution)/shard_map/scatter | solution.py:78
  353.9 9.8 %all-to-all-start = ((s32[32,1,208]{2,1,0:T(1,128)}), s32[32,1,208]{2,1,0:T(1,128)}, u32[]{:S(2)}, u32[]{:S(2)}) async-start(s32[32,1,208]{2,1,0:T(1,128)} %all_to_all.9), calls=%async_computation | async-start | bytes 65536 | tf_op jit(solution)/shard_map/all_to_all | solution.py:83
  363.7 2.6 convert_element_type.18
  369.9 2.1 fusion.10
  376.4 3.3 slice_add_fusion
  379.7 7.8 reshape.231
  387.5 108.6 %scatter_custom_fusion.2 = f32[6657,128]{1,0:T(8,128)S(1)} fusion(s32[13312]{0:T(1024)} %bitcast.63, f32[13312,128]{1,0:T(8,128)} %reshape.231, s32[13312]{0:T(1024)} %fusion.19, f32[]{:T(128)} %constant.21.clone.1), kind=kCustom, calls=%fused_computation.12 | custom fusion | bytes 3408896 | tf_op jit(solution)/shard_map/scatter | solution.py:74
  498.2 7.8 all-to-all-start.1
  511.1 72.4 %scatter_custom_fusion = f32[1025,128]{1,0:T(8,128)} fusion(s32[13312]{0:T(1024)} %bitcast.64, f32[13312,128]{1,0:T(8,128)} %reshape.231, f32[]{:T(128)} %constant.21.clone.1), kind=kCustom, calls=%fused_computation.33 | custom fusion | flops 1703936 | bytes 525312 | tf_op jit(solution)/shard_map/scatter-add | solution.py:58
  588.3 41.0 %scatter_custom_fusion.3 = f32[2048,128]{1,0:T(8,128)} fusion(s32[6656]{0:T(1024)} %reshape.253, f32[6656,128]{1,0:T(8,128)} %bitcast.40, f32[]{:T(128)} %constant.21.clone.1), kind=kCustom, calls=%fused_computation.26 | custom fusion | flops 851968 | bytes 1049088 | tf_op jit(solution)/shard_map/scatter-add | solution.py:85
  629.3 61.0 %all-reduce.9.cloned.1.call-done = f32[1024,128]{1,0:T(8,128)} async-done(((f32[1024,128]{1,0:T(8,128)}), f32[1024,128]{1,0:T(8,128)}) %all-reduce.9.cloned.1.call-update) | async-done | bytes 524304 | tf_op jit(solution)/shard_map/psum | solution.py:90
  690.5 6.2 convolution_bitcast_fusion
  696.7 5.1 fusion.6
  701.8 4.2 fusion.3
  706.0 66.6 %all-reduce.2 = f32[3456]{0:T(1024)} all-reduce(f32[3456]{0:T(1024)S(1)} %fusion.3), channel_id=4, replica_groups=mesh['dp'=32,'rep'=4] {'dp','rep'}, use_global_device_ids=true, to_apply=%region_15.16.clone | all-reduce | flops 3456 | bytes 27648
  779.4 2.3 divide_subtract_fusion.1
  781.7 3.0 divide_subtract_fusion
  784.7 137.9 %all-reduce.11.cloned.1.call-done = (f32[512,3456]{1,0:T(8,128)}, f32[3456,512]{0,1:T(8,128)}) async-done(((f32[512,3456]{1,0:T(8,128)}, f32[3456,512]{0,1:T(8,128)}), (f32[512,3456]{1,0:T(8,128)}, f32[3456,512]{0,1:T(8,128)})) %all-reduce.11.cloned.1.call-update) | async-done | bytes 14155792
  (72 shorter events, 51.4 us)
Async XLA Ops:
  7.2 362.8 %copy-start = (bf16[512,3456]{1,0:T(8,128)(2,1)S(1)}, bf16[512,3456]{1,0:T(8,128)(2,1)}, u32[]{:S(2)}) copy-start(bf16[512,3456]{1,0:T(8,128)(2,1)} %param.13) | copy-start | bytes 10616836
  16.4 0.6 copy-start.2
  353.9 144.3 %all-to-all-start = ((s32[32,1,208]{2,1,0:T(1,128)}), s32[32,1,208]{2,1,0:T(1,128)}, u32[]{:S(2)}, u32[]{:S(2)}) async-start(s32[32,1,208]{2,1,0:T(1,128)} %all_to_all.9), calls=%async_computation | async-start | bytes 65536 | tf_op jit(solution)/shard_map/all_to_all | solution.py:83
  363.7 3.1 copy-start.3
  363.7 4.1 copy-start.7
  367.9 2.1 copy-start.5
  369.9 2.1 copy-start.9
  372.1 4.3 copy-start.11
  372.1 2.2 copy-start.8
  374.3 2.1 copy-start.12
  498.2 192.3 %copy-start.4 = (bf16[512,3456]{1,0:T(8,128)(2,1)S(1)}, bf16[512,3456]{1,0:T(8,128)(2,1)}, u32[]{:S(2)}) copy-start(bf16[512,3456]{1,0:T(8,128)(2,1)} %param.10) | copy-start | bytes 10616836
  498.2 90.1 %all-to-all-start.1 = ((f32[32,208,128]{2,1,0:T(8,128)}), f32[32,208,128]{2,1,0:T(8,128)}, u32[]{:S(2)}, u32[]{:S(2)}) async-start(f32[32,208,128]{2,1,0:T(8,128)} %bitcast.56), calls=%async_computation.1 | async-start | bytes 6815744 | tf_op jit(solution)/shard_map/all_to_all | solution.py:82
  506.1 184.3 %all-reduce.9.cloned.1.call-start = ((), (), s32[]{:S(2)}) async-start(), calls=%async_computation.2 | async-start | bytes 1048576 | tf_op jit(solution)/shard_map/psum | solution.py:90
  585.3 188.6 %all-reduce.13.cloned.1.call-start = ((), (), s32[]{:S(2)}) async-start(), calls=%async_computation.4 | async-start | bytes 3145728 | tf_op jit(solution)/shard_map/psum | solution.py:90
  690.4 232.1 %all-reduce.11.cloned.1.call-start = ((), (), s32[]{:S(2)}) async-start(), calls=%async_computation.3 | async-start | bytes 28311552
  690.5 6.3 copy-start.6
  690.5 6.2 copy-start.10
  701.8 225.9 %copy-start.1 = (bf16[512,3456]{1,0:T(8,128)(2,1)S(1)}, bf16[512,3456]{1,0:T(8,128)(2,1)}, u32[]{:S(2)}) copy-start(bf16[512,3456]{1,0:T(8,128)(2,1)} %param.13) | copy-start | bytes 10616836
Sparse Core Ops, SparseCore 0:
  585.5 104.8 all-reduce.8
  693.5 50.3 all-reduce.12
  749.9 172.6 all-reduce.10
